TPU v7x, 32 devices: a whole 2x2x4 slice. The times are simulated.
32 devices in a mesh: obs: 4 (over z), src: 8 (over y, x, core).
Axes of the slice: x: 2, y: 2, z: 4, core: 2. Of those that a mesh axis runs over, the one named last changes fastest.
Arguments:
- history: bfloat16 [3, 64, 64, 1536], P(None, ('obs', 'src')), may hold values from -6 to 6
- incident: bfloat16 [5, 64, 64, 1536], P(None, ('obs', 'src')), may hold values from -6 to 6
- proj_basis: bfloat16 [64, 64, 1536], P(('obs', 'src')), may hold values from -0.15625 to 0.15625
- expand_basis: bfloat16 [64, 64, 1536], P(('obs', 'src')), may hold values from -0.75 to 0.75
- near_inverse: bfloat16 [64, 1536, 1536], P(('obs', 'src')), may hold values from -0.15625 to 0.15625
- couplings: bfloat16 [2, 4096, 4, 8, 128], P(None, 'obs', None, 'src'), may hold values from -0.09375 to 0.09375
- lags: int32 [64, 4, 8, 2], P('obs', None, 'src'), may hold values from 0 to 2, as said below
Outputs:
- currents: bfloat16 [5, 64, 64, 1536], P(None, ('obs', 'src'))
Inputs may be any that keep to these rules, and one draw needn't show every extreme that they name: lags[j, o, s, k] is the lag from source cluster j to observer cluster (o * 8 + s) * 2 + k. Entries are 0, 1 or 2, and the entry of every cluster with itself is 0.
All inputs are finite; a program needn't handle non-finite values.
Results may differ from a plain program's by a relative error of at most 0.025.
Values may be sent and summed in bfloat16 or wider, within the bound.
A program may use at most 192 MiB of HBM per device.

v0:
```python
import jax
import jax.numpy as jnp
from jax import lax
from jax.sharding import PartitionSpec as P

STEPS = 5
TAPS = 2
HIST = 3


def per_device(history, incident, proj_basis, expand_basis, near_inverse, couplings, lags):
    rank = proj_basis.shape[1]
    local_clusters = proj_basis.shape[0]
    excite = history.shape[2]
    src_rows = couplings.shape[1]
    obs_cols = couplings.shape[2] * couplings.shape[3] * couplings.shape[4]
    src_clusters = lags.shape[0]
    obs_clusters = lags.shape[1] * lags.shape[2] * lags.shape[3]
    kernel = couplings.reshape(TAPS, src_clusters, rank, obs_clusters, rank)
    lag_pairs = lags.reshape(src_clusters, obs_clusters)
    matrices = []
    for delay in range(1, HIST + 1):
        combined = jnp.zeros_like(kernel[0])
        for tap_index in range(TAPS):
            if delay - tap_index >= 1:
                chosen = (lag_pairs == delay - tap_index)[:, None, :, None]
                combined = jnp.where(chosen, kernel[tap_index], combined)
        matrices.append(combined.reshape(src_rows, obs_cols))

    def project(current):
        projected = jnp.einsum(
            "ceb,crb->ecr", current, proj_basis, preferred_element_type=jnp.float32
        )
        return projected.astype(jnp.bfloat16).reshape(excite, local_clusters * rank)

    def couple(columns, delay):
        return jnp.dot(columns, matrices[delay - 1], preferred_element_type=jnp.float32)

    stacked = jnp.stack([project(history[slot_index]) for slot_index in range(HIST)])
    gathered = lax.all_gather(stacked, "src", axis=2, tiled=True)
    past = [gathered[slot_index] for slot_index in range(HIST)]
    results = []
    latest = None
    for step in range(STEPS):
        if step > 0:
            newest = lax.all_gather(latest, "src", axis=1, tiled=True)
            past = past[1:] + [newest]
        partial_value = couple(past[-1], 1) + couple(past[-2], 2) + couple(past[-3], 3)
        field = lax.psum_scatter(
            partial_value.astype(jnp.bfloat16), "obs", scatter_dimension=1, tiled=True
        )
        field_cast = field.reshape(excite, local_clusters, rank)
        far_field = jnp.einsum(
            "ecr,crb->ceb", field_cast, expand_basis, preferred_element_type=jnp.float32
        )
        residual_field = (incident[step].astype(jnp.float32) - far_field).astype(jnp.bfloat16)
        current = jnp.einsum(
            "ceb,cbd->ced", residual_field, near_inverse, preferred_element_type=jnp.float32
        ).astype(jnp.bfloat16)
        results.append(current)
        if step + 1 < STEPS:
            latest = project(current)
    return jnp.stack(results)


def solution(mesh):
    placed = (
        P(None, ("obs", "src"), None, None),
        P(None, ("obs", "src"), None, None),
        P(("obs", "src"), None, None),
        P(("obs", "src"), None, None),
        P(("obs", "src"), None, None),
        P(None, "obs", None, "src", None),
        P("obs", None, "src", None),
    )
    return jax.shard_map(
        per_device,
        mesh=mesh,
        in_specs=placed,
        out_specs=P(None, ("obs", "src"), None, None),
        check_vma=False,
    )
```

profile of v0, /device:TPU:0, one launch (start us, length us, event | category | flops | bytes accessed | tf_op | source)
XLA Modules:
  0.0 237.1 jit_solution(1757093044412803134)
XLA Ops:
  6.5 1.4 convolution_convert_fusion.11
  8.0 1.4 convolution_convert_fusion.10
  9.3 1.4 convolution_convert_fusion.9
  11.1 2.3 fusion.46
  13.3 2.0 squeeze.40
  15.3 1.8 squeeze.42
  17.2 4.3 %select_select_fusion = (bf16[16,64,8,64]{3,2,1,0:T(8,128)(2,1)}, bf16[16,64,8,64]{3,2,1,0:T(8,128)(2,1)}, bf16[16,64,8,64]{3,2,1,0:T(8,128)(2,1)}) fusion(bf16[16,64,8,64]{3,2,1,0:T(8,128)(2,1)} %squeeze.42, bf16[16,64,8,64]{3,2,1,0:T(8,128)(2,1)} %squeeze.40, pred[16,8]{1,0:T(8,128)(4,1)S(1)} %copy.20, pred[16,8]{1,0:T(8,128)(4,1)S(1)} %copy.19, ...), kind=kLoop, calls=%fused_computation.17 | loop fusion | flops 2621440 | bytes 5243264 | tf_op jit(solution)/shard_map/jit(_where)/select_n | solution.py:27
  21.5 4.0 %select_n.97 = bf16[1024,512]{1,0:T(8,128)(2,1)} reshape(bf16[16,64,8,64]{3,2,1,0:T(8,128)(2,1)} %get-tuple-element.7) | data formatting | bytes 2097152 | tf_op jit(solution)/shard_map/jit(_where)/select_n | solution.py:27
  25.6 11.9 %all_gather.15 = bf16[3,64,1024]{1,2,0:T(8,128)(2,1)S(1)} all-gather(bf16[3,64,128]{1,2,0:T(8,128)(2,1)S(1)} %pad_maximum_fusion), channel_id=1, replica_groups=mesh['obs'=4,'src'=8] {'src'}, dimensions={2}, use_global_device_ids=true | all-gather | bytes 442368 | tf_op jit(solution)/shard_map/all_gather | solution.py:40
  37.5 3.5 %select_n.100 = bf16[1024,512]{1,0:T(8,128)(2,1)S(1)} reshape(bf16[16,64,8,64]{3,2,1,0:T(8,128)(2,1)} %get-tuple-element.6) | data formatting | bytes 2097152 | tf_op jit(solution)/shard_map/jit(_where)/select_n | solution.py:27
  41.0 3.2 %select_n.103 = bf16[1024,512]{1,0:T(8,128)(2,1)S(1)} reshape(bf16[16,64,8,64]{3,2,1,0:T(8,128)(2,1)} %get-tuple-element.5) | data formatting | bytes 2097152 | tf_op jit(solution)/shard_map/jit(_where)/select_n | solution.py:27
  44.2 1.5 fusion.42
  45.7 0.3 convolution_add_fusion.7
  46.0 0.3 fusion.11
  46.3 0.8 copy.30
  47.2 1.0 fusion.39
  48.2 0.3 broadcast_in_dim.35
  48.5 2.7 %broadcast_in_dim.38 = pred[1024,512]{1,0:T(32,128)(4,1)} reshape(pred[16,64,8,64]{3,2,1,0:T(8,128)(4,1)S(1)} %broadcast_in_dim.35) | data formatting | bytes 1048576 | tf_op jit(solution)/shard_map/jit(_where)/broadcast_in_dim | solution.py:27
  51.2 0.3 broadcast_in_dim.36
  51.6 2.7 %broadcast_in_dim.39 = pred[1024,512]{1,0:T(32,128)(4,1)} reshape(pred[16,64,8,64]{3,2,1,0:T(8,128)(4,1)S(1)} %broadcast_in_dim.36) | data formatting | bytes 1048576 | tf_op jit(solution)/shard_map/jit(_where)/broadcast_in_dim | solution.py:27
  54.3 2.5 %bitcast_select_fusion.1 = bf16[1024,512]{1,0:T(8,128)(2,1)S(1)} fusion(pred[1024,512]{1,0:T(32,128)(4,1)} %broadcast_in_dim.38, pred[1024,512]{1,0:T(32,128)(4,1)} %broadcast_in_dim.39, bf16[128,8,4,128]{3,2,1,0:T(4,128)(2,1)} %bitcast.199, bf16[128,8,4,128]{3,2,1,0:T(4,128)(2,1)} %bitcast.202), kind=kLoop, calls=%fused_computation.47 | loop fusion | flops 1048576 | bytes 4194304 | tf_op jit(solution)/shard_map/jit(_where)/select_n | solution.py:27
  56.8 1.9 fusion.41
  58.8 8.2 %reduce-scatter.16.cloned.1.call-done = bf16[128,64]{1,0:T(8,128)(2,1)} async-done(((bf16[512,64]{1,0:T(8,128)(2,1)}), bf16[128,64]{1,0:T(8,128)(2,1)}) %reduce-scatter.16.cloned.1.call-update) | async-done | bytes 16400
  67.0 6.7 %bitcast_dynamic-update-slice_fusion.3 = (bf16[5,2,64,1536]{3,2,1,0:T(8,128)(2,1)}, bf16[2,64,1536]{2,1,0:T(8,128)(2,1)}) fusion(bf16[2,1536,1536]{2,1,0:T(8,128)(2,1)} %param.11, bf16[64,2,64]{0,2,1:T(8,128)(2,1)} %bitcast.214, bf16[2,64,1536]{2,1,0:T(8,128)(2,1)S(1)} %copy-done, bf16[5,2,64,1536]{3,2,1,0:T(8,128)(2,1)} %param.8), kind=kOutput, calls=%fused_computation.64 | convolution fusion | flops 629932032 | bytes 11042816 | tf_op jit(solution)/shard_map/ceb,cbd->ced/dot_general | solution.py:57
  73.8 1.4 fusion.14
  75.1 0.6 copy.22
  75.8 0.8 reshape.176
  76.6 9.2 %all_gather.16 = bf16[64,1024]{1,0:T(8,128)(2,1)S(1)} all-gather(bf16[64,128]{1,0:T(8,128)(2,1)S(1)} %reshape.176), channel_id=1, replica_groups=mesh['obs'=4,'src'=8] {'src'}, dimensions={1}, use_global_device_ids=true | all-gather | bytes 147456 | tf_op jit(solution)/shard_map/all_gather | solution.py:46
  85.8 0.6 copy-done.12
  86.5 2.3 fusion.13
  88.7 1.6 copy.32
  90.4 1.9 fusion.40
  92.3 14.9 %reduce-scatter.18.cloned.1.call-done = bf16[128,64]{1,0:T(8,128)(2,1)} async-done(((bf16[512,64]{1,0:T(8,128)(2,1)}), bf16[128,64]{1,0:T(8,128)(2,1)}) %reduce-scatter.18.cloned.1.call-update) | async-done | bytes 16400
  107.2 6.7 %bitcast_dynamic-update-slice_fusion.2 = (bf16[5,2,64,1536]{3,2,1,0:T(8,128)(2,1)}, bf16[2,64,1536]{2,1,0:T(8,128)(2,1)}) fusion(bf16[5,2,64,1536]{3,2,1,0:T(8,128)(2,1)} %get-tuple-element.13, bf16[2,1536,1536]{2,1,0:T(8,128)(2,1)} %param.11, bf16[64,2,64]{0,2,1:T(8,128)(2,1)} %bitcast.216, bf16[2,64,1536]{2,1,0:T(8,128)(2,1)S(1)} %copy-done, ...), kind=kOutput, calls=%fused_computation.63 | convolution fusion | flops 629932032 | bytes 11042816 | tf_op jit(solution)/shard_map/ceb,cbd->ced/dot_general | solution.py:57
  114.0 1.3 fusion.15
  115.3 0.6 copy.24
  115.9 0.8 reshape.178
  116.7 9.1 %all_gather.17 = bf16[64,1024]{1,0:T(8,128)(2,1)S(1)} all-gather(bf16[64,128]{1,0:T(8,128)(2,1)S(1)} %reshape.178), channel_id=1, replica_groups=mesh['obs'=4,'src'=8] {'src'}, dimensions={1}, use_global_device_ids=true | all-gather | bytes 147456 | tf_op jit(solution)/shard_map/all_gather | solution.py:46
  125.9 0.5 fusion.45
  126.8 0.8 copy.34
  127.7 1.3 broadcast_in_dim.37
  129.0 4.0 %broadcast_in_dim.40 = pred[1024,512]{1,0:T(32,128)(4,1)} reshape(pred[16,64,8,64]{3,2,1,0:T(8,128)(4,1)} %broadcast_in_dim.37) | data formatting | bytes 1048576 | tf_op jit(solution)/shard_map/jit(_where)/broadcast_in_dim | solution.py:27
  133.0 11.5 %reduce-scatter.20.cloned.1.call-done = bf16[128,64]{1,0:T(8,128)(2,1)} async-done(((bf16[512,64]{1,0:T(8,128)(2,1)}), bf16[128,64]{1,0:T(8,128)(2,1)}) %reduce-scatter.20.cloned.1.call-update) | async-done | bytes 16400
  144.5 6.6 %bitcast_dynamic-update-slice_fusion.1 = (bf16[5,2,64,1536]{3,2,1,0:T(8,128)(2,1)}, bf16[2,64,1536]{2,1,0:T(8,128)(2,1)S(1)}) fusion(bf16[5,2,64,1536]{3,2,1,0:T(8,128)(2,1)} %get-tuple-element.15, bf16[2,1536,1536]{2,1,0:T(8,128)(2,1)} %param.11, bf16[64,2,64]{0,2,1:T(8,128)(2,1)} %bitcast.215, bf16[2,64,1536]{2,1,0:T(8,128)(2,1)S(1)} %copy-done, ...), kind=kOutput, calls=%fused_computation.62 | convolution fusion | flops 629932032 | bytes 11042816 | tf_op jit(solution)/shard_map/ceb,cbd->ced/dot_general | solution.py:57
  151.3 0.6 copy.26
  152.0 0.9 reshape.180
  152.9 9.1 %all_gather.18 = bf16[64,1024]{1,0:T(8,128)(2,1)S(1)} all-gather(bf16[64,128]{1,0:T(8,128)(2,1)S(1)} %reshape.180), channel_id=1, replica_groups=mesh['obs'=4,'src'=8] {'src'}, dimensions={1}, use_global_device_ids=true | all-gather | bytes 147456 | tf_op jit(solution)/shard_map/all_gather | solution.py:46
  162.1 0.7 copy-done.19
  162.7 1.6 fusion.44
  164.3 0.3 convolution_add_fusion.3
  164.7 1.5 fusion.9
  166.1 1.6 copy.36
  167.8 16.8 %reduce-scatter.22.cloned.1.call-done = bf16[128,64]{1,0:T(8,128)(2,1)} async-done(((bf16[512,64]{1,0:T(8,128)(2,1)}), bf16[128,64]{1,0:T(8,128)(2,1)}) %reduce-scatter.22.cloned.1.call-update) | async-done | bytes 16400
  184.6 6.7 %bitcast_dynamic-update-slice_fusion = (bf16[5,2,64,1536]{3,2,1,0:T(8,128)(2,1)}, bf16[2,64,1536]{2,1,0:T(8,128)(2,1)}) fusion(bf16[5,2,64,1536]{3,2,1,0:T(8,128)(2,1)} %get-tuple-element.17, bf16[2,1536,1536]{2,1,0:T(8,128)(2,1)} %param.11, bf16[64,2,64]{0,2,1:T(8,128)(2,1)} %bitcast.217, bf16[2,64,1536]{2,1,0:T(8,128)(2,1)S(1)} %copy-done, ...), kind=kOutput, calls=%fused_computation.61 | convolution fusion | flops 629932032 | bytes 11042816 | tf_op jit(solution)/shard_map/ceb,cbd->ced/dot_general | solution.py:57
  191.3 1.4 fusion.17
  192.7 0.6 copy.28
  193.3 0.8 reshape.182
  194.2 9.4 %all_gather.19 = bf16[64,1024]{1,0:T(8,128)(2,1)S(1)} all-gather(bf16[64,128]{1,0:T(8,128)(2,1)S(1)} %reshape.182), channel_id=1, replica_groups=mesh['obs'=4,'src'=8] {'src'}, dimensions={1}, use_global_device_ids=true | all-gather | bytes 147456 | tf_op jit(solution)/shard_map/all_gather | solution.py:46
  203.6 1.6 fusion.43
  205.2 0.3 convolution_add_fusion.1
  205.5 0.8 fusion.10
  206.4 0.8 copy.38
  207.1 16.9 %reduce-scatter.24.cloned.1.call-done = bf16[128,64]{1,0:T(8,128)(2,1)} async-done(((bf16[512,64]{1,0:T(8,128)(2,1)}), bf16[128,64]{1,0:T(8,128)(2,1)}) %reduce-scatter.24.cloned.1.call-update) | async-done | bytes 16400
  224.0 6.6 %fusion.6 = bf16[5,2,64,1536]{3,2,1,0:T(8,128)(2,1)} fusion(bf16[5,2,64,1536]{3,2,1,0:T(8,128)(2,1)} %get-tuple-element.19, bf16[2,1536,1536]{2,1,0:T(8,128)(2,1)} %param.11, bf16[64,2,64]{0,2,1:T(8,128)(2,1)} %bitcast.218, bf16[2,64,1536]{2,1,0:T(8,128)(2,1)S(1)} %copy-done, bf16[5,2,64,1536]{3,2,1,0:T(8,128)(2,1)} %param.8), kind=kOutput, calls=%fused_computation.16 | convolution fusion | flops 629932032 | bytes 10649600 | tf_op jit(solution)/shard_map/ceb,cbd->ced/dot_general | solution.py:57
  (66 shorter events, 1.4 us)
Async XLA Ops:
  6.5 60.5 %copy-start = (bf16[2,64,1536]{2,1,0:T(8,128)(2,1)S(1)}, bf16[2,64,1536]{2,1,0:T(8,128)(2,1)}, u32[]{:S(2)}) copy-start(bf16[2,64,1536]{2,1,0:T(8,128)(2,1)} %param.10) | copy-start | bytes 1179652
  6.5 4.2 %copy-start.23 = (s32[16,4,1,2]{0,3,2,1:T(2,128)S(1)}, s32[16,4,1,2]{0,3,2,1:T(2,128)}, u32[]{:S(2)}) copy-start(s32[16,4,1,2]{0,3,2,1:T(2,128)} %param.13) | copy-start | bytes 1540
  6.5 60.5 %reduce-scatter.16.cloned.1.call-start = ((), (), s32[]{:S(2)}) async-start(), calls=%async_computation.5 | async-start | bytes 163840
  11.1 6.1 %copy-start.21 = (pred[16,8]{1,0:T(8,128)(4,1)}, pred[16,8]{1,0:T(8,128)(4,1)S(1)}, u32[]{:S(2)}) copy-start(pred[16,8]{1,0:T(8,128)(4,1)S(1)} %copy.20) | copy-start | bytes 388
  13.3 3.8 %copy-start.1 = (bf16[1,1024,4,1,128]{4,2,3,1,0:T(4,128)(2,1)}, bf16[1,1024,4,1,128]{4,2,3,1,0:T(4,128)(2,1)S(1)}, u32[]{:S(2)}) copy-start(bf16[1,1024,4,1,128]{4,2,3,1,0:T(4,128)(2,1)S(1)} %get-tuple-element.8) | copy-start | bytes 3145732
  13.3 3.8 %copy-start.3 = (bf16[1,1024,4,1,128]{4,2,3,1,0:T(4,128)(2,1)}, bf16[1,1024,4,1,128]{4,2,3,1,0:T(4,128)(2,1)S(1)}, u32[]{:S(2)}) copy-start(bf16[1,1024,4,1,128]{4,2,3,1,0:T(4,128)(2,1)S(1)} %get-tuple-element.9) | copy-start | bytes 3145732
  37.5 9.7 %copy-start.5 = (bf16[3,64,1024]{1,2,0:T(8,128)(2,1)}, bf16[3,64,1024]{1,2,0:T(8,128)(2,1)S(1)}, u32[]{:S(2)}) copy-start(bf16[3,64,1024]{1,2,0:T(8,128)(2,1)S(1)} %all_gather.15) | copy-start | bytes 1179652
  47.1 60.1 %reduce-scatter.18.cloned.1.call-start = ((), (), s32[]{:S(2)}) async-start(), calls=%async_computation.6 | async-start | bytes 163840
  67.0 19.4 %copy-start.4 = (bf16[1,1024,4,1,128]{4,2,3,1,0:T(4,128)(2,1)S(1)}, bf16[1,1024,4,1,128]{4,2,3,1,0:T(4,128)(2,1)}, u32[]{:S(2)}) copy-start(bf16[1,1024,4,1,128]{4,2,3,1,0:T(4,128)(2,1)} %copy-done.3) | copy-start | bytes 3145732
  85.8 0.6 copy-start.12
  90.4 54.2 %reduce-scatter.20.cloned.1.call-start = ((), (), s32[]{:S(2)}) async-start(), calls=%async_computation.7 | async-start | bytes 163840
  107.2 6.8 %copy-start.6 = (bf16[2,64,1536]{2,1,0:T(8,128)(2,1)S(1)}, bf16[2,64,1536]{2,1,0:T(8,128)(2,1)}, u32[]{:S(2)}) copy-start(bf16[2,64,1536]{2,1,0:T(8,128)(2,1)} %param.9) | copy-start | bytes 1179652
  107.2 18.7 %copy-start.9 = (pred[1024,512]{1,0:T(32,128)(4,1)S(1)}, pred[1024,512]{1,0:T(32,128)(4,1)}, u32[]{:S(2)}) copy-start(pred[1024,512]{1,0:T(32,128)(4,1)} %broadcast_in_dim.38) | copy-start | bytes 1572868
  114.0 12.6 %copy-start.13 = (bf16[64,1024]{1,0:T(8,128)(2,1)S(1)}, bf16[64,1024]{1,0:T(8,128)(2,1)}, u32[]{:S(2)}) copy-start(bf16[64,1024]{1,0:T(8,128)(2,1)} %copy-done.12) | copy-start | bytes 393220
  116.7 9.8 %copy-start.15 = (f32[64,512]{1,0:T(8,128)S(1)}, f32[64,512]{1,0:T(8,128)}, u32[]{:S(2)}) copy-start(f32[64,512]{1,0:T(8,128)} %fusion.40) | copy-start | bytes 393220
  125.9 0.7 copy-start.16
  125.9 1.8 copy-start.22
  127.6 57.0 %reduce-scatter.22.cloned.1.call-start = ((), (), s32[]{:S(2)}) async-start(), calls=%async_computation.8 | async-start | bytes 163840
  152.0 12.7 %copy-start.2 = (bf16[1,1024,4,1,128]{4,2,3,1,0:T(4,128)(2,1)S(1)}, bf16[1,1024,4,1,128]{4,2,3,1,0:T(4,128)(2,1)}, u32[]{:S(2)}) copy-start(bf16[1,1024,4,1,128]{4,2,3,1,0:T(4,128)(2,1)} %copy-done.1) | copy-start | bytes 3145732
  152.9 11.4 %copy-start.17 = (bf16[64,1024]{1,0:T(8,128)(2,1)S(1)}, bf16[64,1024]{1,0:T(8,128)(2,1)}, u32[]{:S(2)}) copy-start(bf16[64,1024]{1,0:T(8,128)(2,1)} %copy-done.16) | copy-start | bytes 393220
  152.9 11.7 %copy-start.7 = (pred[1024,512]{1,0:T(32,128)(4,1)S(1)}, pred[1024,512]{1,0:T(32,128)(4,1)}, u32[]{:S(2)}) copy-start(pred[1024,512]{1,0:T(32,128)(4,1)} %broadcast_in_dim.39) | copy-start | bytes 1572868
  152.9 11.7 %copy-start.10 = (pred[1024,512]{1,0:T(32,128)(4,1)S(1)}, pred[1024,512]{1,0:T(32,128)(4,1)}, u32[]{:S(2)}) copy-start(pred[1024,512]{1,0:T(32,128)(4,1)} %broadcast_in_dim.40) | copy-start | bytes 1572868
  152.9 11.7 %copy-start.14 = (bf16[64,1024]{1,0:T(8,128)(2,1)S(1)}, bf16[64,1024]{1,0:T(8,128)(2,1)}, u32[]{:S(2)}) copy-start(bf16[64,1024]{1,0:T(8,128)(2,1)} %copy-done.12) | copy-start | bytes 393220
  162.1 0.7 copy-start.19
  167.8 56.2 %reduce-scatter.24.cloned.1.call-start = ((), (), s32[]{:S(2)}) async-start(), calls=%async_computation.9 | async-start | bytes 163840
  194.1 11.0 %copy-start.20 = (bf16[64,1024]{1,0:T(8,128)(2,1)S(1)}, bf16[64,1024]{1,0:T(8,128)(2,1)}, u32[]{:S(2)}) copy-start(bf16[64,1024]{1,0:T(8,128)(2,1)} %copy-done.19) | copy-start | bytes 393220
  194.1 11.3 %copy-start.8 = (pred[1024,512]{1,0:T(32,128)(4,1)S(1)}, pred[1024,512]{1,0:T(32,128)(4,1)}, u32[]{:S(2)}) copy-start(pred[1024,512]{1,0:T(32,128)(4,1)} %broadcast_in_dim.39) | copy-start | bytes 1572868
  194.2 11.3 %copy-start.11 = (pred[1024,512]{1,0:T(32,128)(4,1)S(1)}, pred[1024,512]{1,0:T(32,128)(4,1)}, u32[]{:S(2)}) copy-start(pred[1024,512]{1,0:T(32,128)(4,1)} %broadcast_in_dim.40) | copy-start | bytes 1572868
  194.2 11.3 %copy-start.18 = (bf16[64,1024]{1,0:T(8,128)(2,1)S(1)}, bf16[64,1024]{1,0:T(8,128)(2,1)}, u32[]{:S(2)}) copy-start(bf16[64,1024]{1,0:T(8,128)(2,1)} %copy-done.16) | copy-start | bytes 393220
Sparse Core Ops, SparseCore 0:
  47.3 19.7 reduce-scatter.15
  90.5 16.6 reduce-scatter.17
  127.7 16.7 reduce-scatter.19
  167.9 16.6 reduce-scatter.21
  207.3 16.6 reduce-scatter.23
where the time goes:
time: 238 us; the launch traced here: 237 us
  waiting for transfers between devices  68.4 us (29%)
  matrix products  57.8 us (24%)
  blocking collectives  48.8 us (21%)
  local copies, waits for them, and re-layouts  41.5 us (17%)
  between operations  13.5 us (6%)
  other arithmetic  6.91 us (3%)
    unnamed x10, waiting for transfers between devices  68.4 us
    all_gather x4, blocking collectives, per_device(): newest = lax.all_gather(latest, 'src', axis=1, tiled=True)  36.9 us
    dot_general x5, matrix products, per_device(): jnp.einsum('ceb,cbd->ced', residual_field, near_inverse, preferred_elemen...  33.3 us
    dot_general x15, matrix products, couple(): jnp.dot(columns, matrices[delay - 1], preferred_element_type=jnp.float32)  16.1 us
    all_gather x1, blocking collectives, per_device(): gathered = lax.all_gather(stacked, 'src', axis=2, tiled=True)  11.9 us
    broadcast_in_dim x6, local copies, waits for them, and re-layouts, per_device(): combined = jnp.where(chosen, kernel[tap_index], combined)  11.4 us
    select_n x3, local copies, waits for them, and re-layouts, per_device(): combined = jnp.where(chosen, kernel[tap_index], combined)  10.7 us
    dot_general x7, matrix products, project(): jnp.einsum('ceb,crb->ecr', current, proj_basis, preferred_element_type=jn...  8.37 us
  transfers between devices with their start and end apart: 5, of which 5 were waited for; matrix products, arithmetic and copies ran while one was open for 8% of the time, Pallas kernels for 0%

commit v1 on v0

--- a/solution.py
+++ b/solution.py
@@ -43,7 +43,26 @@
     latest = None
     for step in range(STEPS):
         if step > 0:
-            newest = lax.all_gather(latest, "src", axis=1, tiled=True)
+            length, here, width = (lax.axis_size("src"), lax.axis_index("src"), latest.shape[1])
+            upward = [(i, (i + 1) % length) for i in range(length)]
+            downward = [(i, (i - 1) % length) for i in range(length)]
+            filled = jnp.zeros(
+                (*latest.shape[:1], length * width, *latest.shape[1 + 1 :]), latest.dtype
+            )
+            filled = lax.dynamic_update_slice_in_dim(filled, latest, here * width, axis=1)
+            from_left = from_right = latest
+            middle = length // 2
+            for hop in range(1, middle + 1):
+                from_left = lax.ppermute(from_left, "src", upward)
+                filled = lax.dynamic_update_slice_in_dim(
+                    filled, from_left, (here - hop) % length * width, axis=1
+                )
+                if hop < length - middle:
+                    from_right = lax.ppermute(from_right, "src", downward)
+                    filled = lax.dynamic_update_slice_in_dim(
+                        filled, from_right, (here + hop) % length * width, axis=1
+                    )
+            newest = filled
             past = past[1:] + [newest]
         partial_value = couple(past[-1], 1) + couple(past[-2], 2) + couple(past[-3], 3)
         field = lax.psum_scatter(

time: 238 us -> 259 us (1.088)
  blocking collectives: 48.8 us -> 11.9 us
  starting transfers between devices: 0.17 us -> 32.5 us
  waiting for transfers between devices: 68.4 us -> 99.3 us
  local copies, waits for them, and re-layouts: 41.5 us -> 32.1 us
  matrix products: 57.8 us -> 62.4 us
    all_gather x4 -> x0, blocking collectives: 36.9 us -> none  [per_device(): newest = lax.all_gather(latest, 'src', axis=1, tiled=True)]
    ppermute x0 -> x28, waiting for transfers between devices: none -> 32.9 us  [the longest x16 32.3 us: per_device(): from_left = lax.ppermute(from_left, 'src', upward)]
    ppermute x0 -> x28, starting transfers between devices: none -> 31.9 us  [the longest x12 31.7 us: per_device(): from_right = lax.ppermute(from_right, 'src', downward)]
    dot_general x15, matrix products: 16.1 us -> 20.6 us  [couple(): jnp.dot(columns, matrices[delay - 1], preferred_element_type=jnp.float32)]
    broadcast_in_dim x6, local copies, waits for them, and re-layouts: 11.4 us -> 7.93 us  [per_device(): combined = jnp.where(chosen, kernel[tap_index], combined)]
    unnamed x53 -> x31, local copies, waits for them, and re-layouts: 6.97 us -> 6.99 us
  transfers between devices with their start and end apart: 5 -> 33, of which waited for: 5 -> 27; matrix products, arithmetic and copies ran while one was open for 8% -> 8% of each run, Pallas kernels for 0% -> 0%
where the time goes in v1:
time: 259 us; the launch traced here: 258 us
  waiting for transfers between devices  99.3 us (38%)
  matrix products  62.4 us (24%)
  starting transfers between devices  32.5 us (13%)
  local copies, waits for them, and re-layouts  32.1 us (12%)
  between operations  13.5 us (5%)
  blocking collectives  11.9 us (5%)
  other arithmetic  6.51 us (3%)
    unnamed x10, waiting for transfers between devices  66.4 us
    dot_general x5, matrix products, per_device(): jnp.einsum('ceb,cbd->ced', residual_field, near_inverse, preferred_elemen...  33.3 us
    ppermute x16, waiting for transfers between devices, per_device(): from_left = lax.ppermute(from_left, 'src', upward)  32.3 us
    ppermute x12, starting transfers between devices, per_device(): from_right = lax.ppermute(from_right, 'src', downward)  31.7 us
    dot_general x15, matrix products, couple(): jnp.dot(columns, matrices[delay - 1], preferred_element_type=jnp.float32)  20.6 us
    all_gather x1, blocking collectives, per_device(): gathered = lax.all_gather(stacked, 'src', axis=2, tiled=True)  11.9 us
    select_n x3, local copies, waits for them, and re-layouts, per_device(): combined = jnp.where(chosen, kernel[tap_index], combined)  8.7 us
    dot_general x7, matrix products, project(): jnp.einsum('ceb,crb->ecr', current, proj_basis, preferred_element_type=jn...  8.42 us
  transfers between devices with their start and end apart: 33, of which 27 were waited for; matrix products, arithmetic and copies ran while one was open for 8% of the time, Pallas kernels for 0%

profile of v1, /device:TPU:0, one launch (start us, length us, event | category | flops | bytes accessed | tf_op | source)
XLA Modules:
  0.0 258.1 jit_solution(1248480103618327704)
XLA Ops:
  6.5 1.5 convolution_convert_fusion.9
  8.1 1.4 convolution_convert_fusion.10
  9.4 1.4 convolution_convert_fusion.11
  11.6 2.0 squeeze.42
  13.6 1.8 squeeze.40
  15.8 3.8 %select_select_fusion = (bf16[16,64,8,64]{3,2,1,0:T(8,128)(2,1)}, bf16[16,64,8,64]{3,2,1,0:T(8,128)(2,1)}, bf16[16,64,8,64]{3,2,1,0:T(8,128)(2,1)S(1)}) fusion(bf16[16,64,8,64]{3,2,1,0:T(8,128)(2,1)} %squeeze.42, bf16[16,64,8,64]{3,2,1,0:T(8,128)(2,1)} %squeeze.40, pred[16,8]{1,0:T(8,128)(4,1)S(1)} %copy.20, pred[16,8]{1,0:T(8,128)(4,1)S(1)} %copy.19, ...), kind=kLoop, calls=%fused_computation.17 | loop fusion | flops 2621440 | bytes 5243264 | tf_op jit(solution)/shard_map/jit(_where)/select_n | solution.py:27
  19.6 2.0 select_n.218
  21.6 11.9 %all_gather.3 = bf16[3,64,1024]{1,2,0:T(8,128)(2,1)S(1)} all-gather(bf16[3,64,128]{1,2,0:T(8,128)(2,1)S(1)} %pad_maximum_fusion), channel_id=1, replica_groups=mesh['obs'=4,'src'=8] {'src'}, dimensions={2}, use_global_device_ids=true | all-gather | bytes 442368 | tf_op jit(solution)/shard_map/all_gather | solution.py:40
  33.5 3.5 %select_n.221 = bf16[1024,512]{1,0:T(8,128)(2,1)S(1)} reshape(bf16[16,64,8,64]{3,2,1,0:T(8,128)(2,1)} %get-tuple-element.6) | data formatting | bytes 2097152 | tf_op jit(solution)/shard_map/jit(_where)/select_n | solution.py:27
  37.0 3.2 %select_n.224 = bf16[1024,512]{1,0:T(8,128)(2,1)S(1)} reshape(bf16[16,64,8,64]{3,2,1,0:T(8,128)(2,1)} %get-tuple-element.5) | data formatting | bytes 2097152 | tf_op jit(solution)/shard_map/jit(_where)/select_n | solution.py:27
  40.2 1.5 fusion.44
  45.7 2.7 %broadcast_in_dim.38 = pred[1024,512]{1,0:T(32,128)(4,1)} reshape(pred[16,64,8,64]{3,2,1,0:T(8,128)(4,1)S(1)} %broadcast_in_dim.35) | data formatting | bytes 1048576 | tf_op jit(solution)/shard_map/jit(_where)/broadcast_in_dim | solution.py:27
  48.8 2.1 broadcast_in_dim.39
  51.2 2.1 broadcast_in_dim.40
  53.3 2.7 %bitcast_select_fusion = (bf16[1024,512]{1,0:T(8,128)(2,1)S(1)}, bf16[1024,512]{1,0:T(8,128)(2,1)S(1)}) fusion(pred[1024,512]{1,0:T(8,128)(4,1)} %broadcast_in_dim.39, pred[1024,512]{1,0:T(8,128)(4,1)} %broadcast_in_dim.40, bf16[128,8,4,128]{3,2,1,0:T(4,128)(2,1)} %bitcast.202, bf16[128,8,4,128]{3,2,1,0:T(4,128)(2,1)} %bitcast.197, ...), kind=kLoop, calls=%fused_computation.46 | loop fusion | flops 2097152 | bytes 5767168 | tf_op jit(solution)/shard_map/jit(_where)/select_n | solution.py:27
  56.0 1.9 fusion.42
  57.9 5.2 %reduce-scatter.16.cloned.1.call-done = bf16[128,64]{1,0:T(8,128)(2,1)} async-done(((bf16[512,64]{1,0:T(8,128)(2,1)}), bf16[128,64]{1,0:T(8,128)(2,1)}) %reduce-scatter.16.cloned.1.call-update) | async-done | bytes 16400
  63.1 6.8 %bitcast_dynamic-update-slice_fusion.3 = (bf16[5,2,64,1536]{3,2,1,0:T(8,128)(2,1)}, bf16[2,64,1536]{2,1,0:T(8,128)(2,1)}) fusion(bf16[2,1536,1536]{2,1,0:T(8,128)(2,1)} %param.11, bf16[64,2,64]{0,2,1:T(8,128)(2,1)} %bitcast.208, bf16[2,64,1536]{2,1,0:T(8,128)(2,1)S(1)} %copy-done, bf16[5,2,64,1536]{3,2,1,0:T(8,128)(2,1)} %param.8), kind=kOutput, calls=%fused_computation.64 | convolution fusion | flops 629932032 | bytes 11042816 | tf_op jit(solution)/shard_map/ceb,cbd->ced/dot_general | solution.py:76
  69.8 1.4 fusion.16
  72.7 2.6 %collective-permute-start.1 = (bf16[64,128]{1,0:T(8,128)(2,1)S(1)}, bf16[64,128]{1,0:T(8,128)(2,1)S(1)}, u32[]{:S(2)}, u32[]{:S(2)}) collective-permute-start(bf16[64,128]{1,0:T(8,128)(2,1)S(1)} %reshape.176), channel_id=1, source_target_pairs={{0,7},{1,0},{2,1},{3,2},{4,3},{5,4},{6,5},{7,6},{8,15},{9,8},{10,9... | collective-permute-start | bytes 49160 | tf_op jit(solution)/shard_map/ppermute | solution.py:61
  75.4 1.4 collective-permute-done
  76.8 2.6 %collective-permute-start.3 = (bf16[64,128]{1,0:T(8,128)(2,1)S(1)}, bf16[64,128]{1,0:T(8,128)(2,1)S(1)}, u32[]{:S(2)}, u32[]{:S(2)}) collective-permute-start(bf16[64,128]{1,0:T(8,128)(2,1)S(1)} %collective-permute-done.1), channel_id=1, source_target_pairs={{0,7},{1,0},{2,1},{3,2},{4,3},{5,4},{6,5},{7,6},{8,15},{9,8},{10,9... | collective-permute-start | bytes 49160 | tf_op jit(solution)/shard_map/ppermute | solution.py:61
  79.5 1.4 collective-permute-done.2
  80.9 2.6 %collective-permute-start.5 = (bf16[64,128]{1,0:T(8,128)(2,1)S(1)}, bf16[64,128]{1,0:T(8,128)(2,1)S(1)}, u32[]{:S(2)}, u32[]{:S(2)}) collective-permute-start(bf16[64,128]{1,0:T(8,128)(2,1)S(1)} %collective-permute-done.3), channel_id=1, source_target_pairs={{0,7},{1,0},{2,1},{3,2},{4,3},{5,4},{6,5},{7,6},{8,15},{9,8},{10,9... | collective-permute-start | bytes 49160 | tf_op jit(solution)/shard_map/ppermute | solution.py:61
  83.5 1.4 collective-permute-done.4
  85.0 4.0 %collective-permute-done.6 = bf16[64,128]{1,0:T(8,128)(2,1)S(1)} collective-permute-done((bf16[64,128]{1,0:T(8,128)(2,1)S(1)}, bf16[64,128]{1,0:T(8,128)(2,1)S(1)}, u32[]{:S(2)}, u32[]{:S(2)}) %collective-permute-start.6) | collective-permute-done | bytes 16416 | tf_op jit(solution)/shard_map/ppermute | solution.py:56
  89.6 2.3 fusion.15
  91.9 1.6 copy.32
  93.6 1.8 fusion.46
  95.4 1.9 fusion.48
  97.3 13.3 %reduce-scatter.18.cloned.1.call-done = bf16[128,64]{1,0:T(8,128)(2,1)} async-done(((bf16[512,64]{1,0:T(8,128)(2,1)}), bf16[128,64]{1,0:T(8,128)(2,1)}) %reduce-scatter.18.cloned.1.call-update) | async-done | bytes 16400
  110.6 6.7 %bitcast_dynamic-update-slice_fusion.2 = (bf16[5,2,64,1536]{3,2,1,0:T(8,128)(2,1)}, bf16[2,64,1536]{2,1,0:T(8,128)(2,1)}) fusion(bf16[5,2,64,1536]{3,2,1,0:T(8,128)(2,1)} %get-tuple-element.15, bf16[2,1536,1536]{2,1,0:T(8,128)(2,1)} %param.11, bf16[64,2,64]{0,2,1:T(8,128)(2,1)} %bitcast.209, bf16[2,64,1536]{2,1,0:T(8,128)(2,1)S(1)} %copy-done, ...), kind=kOutput, calls=%fused_computation.63 | convolution fusion | flops 629932032 | bytes 11042816 | tf_op jit(solution)/shard_map/ceb,cbd->ced/dot_general | solution.py:76
  117.2 1.4 fusion.17
  120.2 2.6 %collective-permute-start.8 = (bf16[64,128]{1,0:T(8,128)(2,1)S(1)}, bf16[64,128]{1,0:T(8,128)(2,1)S(1)}, u32[]{:S(2)}, u32[]{:S(2)}) collective-permute-start(bf16[64,128]{1,0:T(8,128)(2,1)S(1)} %reshape.178), channel_id=1, source_target_pairs={{0,7},{1,0},{2,1},{3,2},{4,3},{5,4},{6,5},{7,6},{8,15},{9,8},{10,9... | collective-permute-start | bytes 49160 | tf_op jit(solution)/shard_map/ppermute | solution.py:61
  122.8 1.4 collective-permute-done.7
  124.2 2.7 %collective-permute-start.10 = (bf16[64,128]{1,0:T(8,128)(2,1)S(1)}, bf16[64,128]{1,0:T(8,128)(2,1)S(1)}, u32[]{:S(2)}, u32[]{:S(2)}) collective-permute-start(bf16[64,128]{1,0:T(8,128)(2,1)S(1)} %collective-permute-done.8), channel_id=1, source_target_pairs={{0,7},{1,0},{2,1},{3,2},{4,3},{5,4},{6,5},{7,6},{8,15},{9,8},{10,9... | collective-permute-start | bytes 49160 | tf_op jit(solution)/shard_map/ppermute | solution.py:61
  126.9 1.3 collective-permute-done.9
  128.4 2.6 %collective-permute-start.12 = (bf16[64,128]{1,0:T(8,128)(2,1)S(1)}, bf16[64,128]{1,0:T(8,128)(2,1)S(1)}, u32[]{:S(2)}, u32[]{:S(2)}) collective-permute-start(bf16[64,128]{1,0:T(8,128)(2,1)S(1)} %collective-permute-done.10), channel_id=1, source_target_pairs={{0,7},{1,0},{2,1},{3,2},{4,3},{5,4},{6,5},{7,6},{8,15},{9,8},{10,9... | collective-permute-start | bytes 49160 | tf_op jit(solution)/shard_map/ppermute | solution.py:61
  131.0 1.3 collective-permute-done.11
  132.4 4.0 %collective-permute-done.13 = bf16[64,128]{1,0:T(8,128)(2,1)S(1)} collective-permute-done((bf16[64,128]{1,0:T(8,128)(2,1)S(1)}, bf16[64,128]{1,0:T(8,128)(2,1)S(1)}, u32[]{:S(2)}, u32[]{:S(2)}) %collective-permute-start.13) | collective-permute-done | bytes 16416 | tf_op jit(solution)/shard_map/ppermute | solution.py:56
  137.4 2.3 fusion.14
  139.6 1.6 copy.34
  141.5 1.8 fusion.50
  143.4 14.8 %reduce-scatter.20.cloned.1.call-done = bf16[128,64]{1,0:T(8,128)(2,1)} async-done(((bf16[512,64]{1,0:T(8,128)(2,1)}), bf16[128,64]{1,0:T(8,128)(2,1)}) %reduce-scatter.20.cloned.1.call-update) | async-done | bytes 16400
  158.2 6.7 %bitcast_dynamic-update-slice_fusion.1 = (bf16[5,2,64,1536]{3,2,1,0:T(8,128)(2,1)}, bf16[2,64,1536]{2,1,0:T(8,128)(2,1)}) fusion(bf16[5,2,64,1536]{3,2,1,0:T(8,128)(2,1)} %get-tuple-element.17, bf16[2,1536,1536]{2,1,0:T(8,128)(2,1)} %param.11, bf16[64,2,64]{0,2,1:T(8,128)(2,1)} %bitcast.210, bf16[2,64,1536]{2,1,0:T(8,128)(2,1)S(1)} %copy-done, ...), kind=kOutput, calls=%fused_computation.62 | convolution fusion | flops 629932032 | bytes 11042816 | tf_op jit(solution)/shard_map/ceb,cbd->ced/dot_general | solution.py:76
  166.4 2.6 %collective-permute-start.15 = (bf16[64,128]{1,0:T(8,128)(2,1)S(1)}, bf16[64,128]{1,0:T(8,128)(2,1)S(1)}, u32[]{:S(2)}, u32[]{:S(2)}) collective-permute-start(bf16[64,128]{1,0:T(8,128)(2,1)S(1)} %reshape.180), channel_id=1, source_target_pairs={{0,7},{1,0},{2,1},{3,2},{4,3},{5,4},{6,5},{7,6},{8,15},{9,8},{10,9... | collective-permute-start | bytes 49160 | tf_op jit(solution)/shard_map/ppermute | solution.py:61
  169.1 1.4 collective-permute-done.14
  170.5 2.7 %collective-permute-start.17 = (bf16[64,128]{1,0:T(8,128)(2,1)S(1)}, bf16[64,128]{1,0:T(8,128)(2,1)S(1)}, u32[]{:S(2)}, u32[]{:S(2)}) collective-permute-start(bf16[64,128]{1,0:T(8,128)(2,1)S(1)} %collective-permute-done.15), channel_id=1, source_target_pairs={{0,7},{1,0},{2,1},{3,2},{4,3},{5,4},{6,5},{7,6},{8,15},{9,8},{10,9... | collective-permute-start | bytes 49160 | tf_op jit(solution)/shard_map/ppermute | solution.py:61
  173.2 1.3 collective-permute-done.16
  174.6 2.6 %collective-permute-start.19 = (bf16[64,128]{1,0:T(8,128)(2,1)S(1)}, bf16[64,128]{1,0:T(8,128)(2,1)S(1)}, u32[]{:S(2)}, u32[]{:S(2)}) collective-permute-start(bf16[64,128]{1,0:T(8,128)(2,1)S(1)} %collective-permute-done.17), channel_id=1, source_target_pairs={{0,7},{1,0},{2,1},{3,2},{4,3},{5,4},{6,5},{7,6},{8,15},{9,8},{10,9... | collective-permute-start | bytes 49160 | tf_op jit(solution)/shard_map/ppermute | solution.py:61
  177.2 1.3 collective-permute-done.18
  178.7 4.0 %collective-permute-done.20 = bf16[64,128]{1,0:T(8,128)(2,1)S(1)} collective-permute-done((bf16[64,128]{1,0:T(8,128)(2,1)S(1)}, bf16[64,128]{1,0:T(8,128)(2,1)S(1)}, u32[]{:S(2)}, u32[]{:S(2)}) %collective-permute-start.20) | collective-permute-done | bytes 16416 | tf_op jit(solution)/shard_map/ppermute | solution.py:56
  182.6 2.1 fusion.13
  184.8 1.6 copy.36
  187.4 16.0 %reduce-scatter.22.cloned.1.call-done = bf16[128,64]{1,0:T(8,128)(2,1)} async-done(((bf16[512,64]{1,0:T(8,128)(2,1)}), bf16[128,64]{1,0:T(8,128)(2,1)}) %reduce-scatter.22.cloned.1.call-update) | async-done | bytes 16400
  203.4 6.6 %bitcast_dynamic-update-slice_fusion = (bf16[5,2,64,1536]{3,2,1,0:T(8,128)(2,1)}, bf16[2,64,1536]{2,1,0:T(8,128)(2,1)S(1)}) fusion(bf16[5,2,64,1536]{3,2,1,0:T(8,128)(2,1)} %get-tuple-element.19, bf16[2,1536,1536]{2,1,0:T(8,128)(2,1)} %param.11, bf16[64,2,64]{0,2,1:T(8,128)(2,1)} %bitcast.211, bf16[2,64,1536]{2,1,0:T(8,128)(2,1)S(1)} %copy-done, ...), kind=kOutput, calls=%fused_computation.61 | convolution fusion | flops 629932032 | bytes 11042816 | tf_op jit(solution)/shard_map/ceb,cbd->ced/dot_general | solution.py:76
  210.4 2.6 %collective-permute-start.22 = (bf16[64,128]{1,0:T(8,128)(2,1)S(1)}, bf16[64,128]{1,0:T(8,128)(2,1)S(1)}, u32[]{:S(2)}, u32[]{:S(2)}) collective-permute-start(bf16[64,128]{1,0:T(8,128)(2,1)S(1)} %reshape.182), channel_id=1, source_target_pairs={{0,7},{1,0},{2,1},{3,2},{4,3},{5,4},{6,5},{7,6},{8,15},{9,8},{10,9... | collective-permute-start | bytes 49160 | tf_op jit(solution)/shard_map/ppermute | solution.py:61
  213.1 1.4 collective-permute-done.21
  214.5 2.7 %collective-permute-start.24 = (bf16[64,128]{1,0:T(8,128)(2,1)S(1)}, bf16[64,128]{1,0:T(8,128)(2,1)S(1)}, u32[]{:S(2)}, u32[]{:S(2)}) collective-permute-start(bf16[64,128]{1,0:T(8,128)(2,1)S(1)} %collective-permute-done.22), channel_id=1, source_target_pairs={{0,7},{1,0},{2,1},{3,2},{4,3},{5,4},{6,5},{7,6},{8,15},{9,8},{10,9... | collective-permute-start | bytes 49160 | tf_op jit(solution)/shard_map/ppermute | solution.py:61
  217.2 1.3 collective-permute-done.23
  218.6 2.6 %collective-permute-start.26 = (bf16[64,128]{1,0:T(8,128)(2,1)S(1)}, bf16[64,128]{1,0:T(8,128)(2,1)S(1)}, u32[]{:S(2)}, u32[]{:S(2)}) collective-permute-start(bf16[64,128]{1,0:T(8,128)(2,1)S(1)} %collective-permute-done.24), channel_id=1, source_target_pairs={{0,7},{1,0},{2,1},{3,2},{4,3},{5,4},{6,5},{7,6},{8,15},{9,8},{10,9... | collective-permute-start | bytes 49160 | tf_op jit(solution)/shard_map/ppermute | solution.py:61
  222.7 4.0 %collective-permute-done.27 = bf16[64,128]{1,0:T(8,128)(2,1)S(1)} collective-permute-done((bf16[64,128]{1,0:T(8,128)(2,1)S(1)}, bf16[64,128]{1,0:T(8,128)(2,1)S(1)}, u32[]{:S(2)}, u32[]{:S(2)}) %collective-permute-start.27) | collective-permute-done | bytes 16416 | tf_op jit(solution)/shard_map/ppermute | solution.py:56
  228.0 17.1 %reduce-scatter.24.cloned.1.call-done = bf16[128,64]{1,0:T(8,128)(2,1)} async-done(((bf16[512,64]{1,0:T(8,128)(2,1)}), bf16[128,64]{1,0:T(8,128)(2,1)}) %reduce-scatter.24.cloned.1.call-update) | async-done | bytes 16400
  245.1 6.5 %fusion.6 = bf16[5,2,64,1536]{3,2,1,0:T(8,128)(2,1)} fusion(bf16[5,2,64,1536]{3,2,1,0:T(8,128)(2,1)} %get-tuple-element.21, bf16[2,1536,1536]{2,1,0:T(8,128)(2,1)} %param.11, bf16[64,2,64]{0,2,1:T(8,128)(2,1)} %bitcast.212, bf16[2,64,1536]{2,1,0:T(8,128)(2,1)S(1)} %copy-done, bf16[5,2,64,1536]{3,2,1,0:T(8,128)(2,1)} %param.8), kind=kOutput, calls=%fused_computation.16 | convolution fusion | flops 629932032 | bytes 10649600 | tf_op jit(solution)/shard_map/ceb,cbd->ced/dot_general | solution.py:76
  (132 shorter events, 17.2 us)
Async XLA Ops:
  6.5 56.5 %copy-start = (bf16[2,64,1536]{2,1,0:T(8,128)(2,1)S(1)}, bf16[2,64,1536]{2,1,0:T(8,128)(2,1)}, u32[]{:S(2)}) copy-start(bf16[2,64,1536]{2,1,0:T(8,128)(2,1)} %param.10) | copy-start | bytes 1179652
  6.5 56.5 %reduce-scatter.16.cloned.1.call-start = ((), (), s32[]{:S(2)}) async-start(), calls=%async_computation.5 | async-start | bytes 163840
  6.5 4.3 %copy-start.6 = (bf16[2,1024,4,1,128]{4,2,3,1,0:T(4,128)(2,1)S(1)}, bf16[2,1024,4,1,128]{4,2,3,1,0:T(4,128)(2,1)}, u32[]{:S(2)}) copy-start(bf16[2,1024,4,1,128]{4,2,3,1,0:T(4,128)(2,1)} %param.12) | copy-start | bytes 6291460
  11.5 3.9 %copy-start.1 = (bf16[1,1024,4,1,128]{4,2,3,1,0:T(4,128)(2,1)}, bf16[1,1024,4,1,128]{4,2,3,1,0:T(4,128)(2,1)S(1)}, u32[]{:S(2)}) copy-start(bf16[1,1024,4,1,128]{4,2,3,1,0:T(4,128)(2,1)S(1)} %get-tuple-element.11) | copy-start | bytes 3145732
  11.5 3.9 %copy-start.3 = (bf16[1,1024,4,1,128]{4,2,3,1,0:T(4,128)(2,1)}, bf16[1,1024,4,1,128]{4,2,3,1,0:T(4,128)(2,1)S(1)}, u32[]{:S(2)}) copy-start(bf16[1,1024,4,1,128]{4,2,3,1,0:T(4,128)(2,1)S(1)} %get-tuple-element.10) | copy-start | bytes 3145732
  13.6 1.8 copy-start.12
  33.5 10.9 %copy-start.4 = (bf16[3,64,1024]{1,2,0:T(8,128)(2,1)}, bf16[3,64,1024]{1,2,0:T(8,128)(2,1)S(1)}, u32[]{:S(2)}) copy-start(bf16[3,64,1024]{1,2,0:T(8,128)(2,1)S(1)} %all_gather.3) | copy-start | bytes 1179652
  43.2 67.4 %reduce-scatter.18.cloned.1.call-start = ((), (), s32[]{:S(2)}) async-start(), calls=%async_computation.6 | async-start | bytes 163840
  63.1 26.6 %copy-start.2 = (bf16[1,1024,4,1,128]{4,2,3,1,0:T(4,128)(2,1)S(1)}, bf16[1,1024,4,1,128]{4,2,3,1,0:T(4,128)(2,1)}, u32[]{:S(2)}) copy-start(bf16[1,1024,4,1,128]{4,2,3,1,0:T(4,128)(2,1)} %copy-done.1) | copy-start | bytes 3145732
  72.7 4.1 %collective-permute-start = (bf16[64,128]{1,0:T(8,128)(2,1)S(1)}, bf16[64,128]{1,0:T(8,128)(2,1)S(1)}, u32[]{:S(2)}, u32[]{:S(2)}) collective-permute-start(bf16[64,128]{1,0:T(8,128)(2,1)S(1)} %reshape.176), channel_id=1, source_target_pairs={{0,1},{1,2},{2,3},{3,4},{4,5},{5,6},{6,7},{7,0},{8,9},{9,10},{10,1... | collective-permute-start | bytes 49160 | tf_op jit(solution)/shard_map/ppermute | solution.py:56
  72.7 4.1 %collective-permute-start.1 = (bf16[64,128]{1,0:T(8,128)(2,1)S(1)}, bf16[64,128]{1,0:T(8,128)(2,1)S(1)}, u32[]{:S(2)}, u32[]{:S(2)}) collective-permute-start(bf16[64,128]{1,0:T(8,128)(2,1)S(1)} %reshape.176), channel_id=1, source_target_pairs={{0,7},{1,0},{2,1},{3,2},{4,3},{5,4},{6,5},{7,6},{8,15},{9,8},{10,9... | collective-permute-start | bytes 49160 | tf_op jit(solution)/shard_map/ppermute | solution.py:61
  76.8 4.1 %collective-permute-start.2 = (bf16[64,128]{1,0:T(8,128)(2,1)S(1)}, bf16[64,128]{1,0:T(8,128)(2,1)S(1)}, u32[]{:S(2)}, u32[]{:S(2)}) collective-permute-start(bf16[64,128]{1,0:T(8,128)(2,1)S(1)} %collective-permute-done), channel_id=1, source_target_pairs={{0,1},{1,2},{2,3},{3,4},{4,5},{5,6},{6,7},{7,0},{8,9},{9,10},{10,1... | collective-permute-start | bytes 49160 | tf_op jit(solution)/shard_map/ppermute | solution.py:56
  76.8 4.1 %collective-permute-start.3 = (bf16[64,128]{1,0:T(8,128)(2,1)S(1)}, bf16[64,128]{1,0:T(8,128)(2,1)S(1)}, u32[]{:S(2)}, u32[]{:S(2)}) collective-permute-start(bf16[64,128]{1,0:T(8,128)(2,1)S(1)} %collective-permute-done.1), channel_id=1, source_target_pairs={{0,7},{1,0},{2,1},{3,2},{4,3},{5,4},{6,5},{7,6},{8,15},{9,8},{10,9... | collective-permute-start | bytes 49160 | tf_op jit(solution)/shard_map/ppermute | solution.py:61
  80.9 4.1 %collective-permute-start.4 = (bf16[64,128]{1,0:T(8,128)(2,1)S(1)}, bf16[64,128]{1,0:T(8,128)(2,1)S(1)}, u32[]{:S(2)}, u32[]{:S(2)}) collective-permute-start(bf16[64,128]{1,0:T(8,128)(2,1)S(1)} %collective-permute-done.2), channel_id=1, source_target_pairs={{0,1},{1,2},{2,3},{3,4},{4,5},{5,6},{6,7},{7,0},{8,9},{9,10},{10,1... | collective-permute-start | bytes 49160 | tf_op jit(solution)/shard_map/ppermute | solution.py:56
  80.9 4.1 %collective-permute-start.5 = (bf16[64,128]{1,0:T(8,128)(2,1)S(1)}, bf16[64,128]{1,0:T(8,128)(2,1)S(1)}, u32[]{:S(2)}, u32[]{:S(2)}) collective-permute-start(bf16[64,128]{1,0:T(8,128)(2,1)S(1)} %collective-permute-done.3), channel_id=1, source_target_pairs={{0,7},{1,0},{2,1},{3,2},{4,3},{5,4},{6,5},{7,6},{8,15},{9,8},{10,9... | collective-permute-start | bytes 49160 | tf_op jit(solution)/shard_map/ppermute | solution.py:61
  84.9 4.1 %collective-permute-start.6 = (bf16[64,128]{1,0:T(8,128)(2,1)S(1)}, bf16[64,128]{1,0:T(8,128)(2,1)S(1)}, u32[]{:S(2)}, u32[]{:S(2)}) collective-permute-start(bf16[64,128]{1,0:T(8,128)(2,1)S(1)} %collective-permute-done.4), channel_id=1, source_target_pairs={{0,1},{1,2},{2,3},{3,4},{4,5},{5,6},{6,7},{7,0},{8,9},{9,10},{10,1... | collective-permute-start | bytes 49160 | tf_op jit(solution)/shard_map/ppermute | solution.py:56
  89.0 0.7 copy-start.8
  93.5 64.7 %reduce-scatter.20.cloned.1.call-start = ((), (), s32[]{:S(2)}) async-start(), calls=%async_computation.7 | async-start | bytes 163840
  120.1 4.1 %collective-permute-start.7 = (bf16[64,128]{1,0:T(8,128)(2,1)S(1)}, bf16[64,128]{1,0:T(8,128)(2,1)S(1)}, u32[]{:S(2)}, u32[]{:S(2)}) collective-permute-start(bf16[64,128]{1,0:T(8,128)(2,1)S(1)} %reshape.178), channel_id=1, source_target_pairs={{0,1},{1,2},{2,3},{3,4},{4,5},{5,6},{6,7},{7,0},{8,9},{9,10},{10,1... | collective-permute-start | bytes 49160 | tf_op jit(solution)/shard_map/ppermute | solution.py:56
  120.2 4.1 %collective-permute-start.8 = (bf16[64,128]{1,0:T(8,128)(2,1)S(1)}, bf16[64,128]{1,0:T(8,128)(2,1)S(1)}, u32[]{:S(2)}, u32[]{:S(2)}) collective-permute-start(bf16[64,128]{1,0:T(8,128)(2,1)S(1)} %reshape.178), channel_id=1, source_target_pairs={{0,7},{1,0},{2,1},{3,2},{4,3},{5,4},{6,5},{7,6},{8,15},{9,8},{10,9... | collective-permute-start | bytes 49160 | tf_op jit(solution)/shard_map/ppermute | solution.py:61
  124.2 4.1 %collective-permute-start.9 = (bf16[64,128]{1,0:T(8,128)(2,1)S(1)}, bf16[64,128]{1,0:T(8,128)(2,1)S(1)}, u32[]{:S(2)}, u32[]{:S(2)}) collective-permute-start(bf16[64,128]{1,0:T(8,128)(2,1)S(1)} %collective-permute-done.7), channel_id=1, source_target_pairs={{0,1},{1,2},{2,3},{3,4},{4,5},{5,6},{6,7},{7,0},{8,9},{9,10},{10,1... | collective-permute-start | bytes 49160 | tf_op jit(solution)/shard_map/ppermute | solution.py:56
  124.2 4.1 %collective-permute-start.10 = (bf16[64,128]{1,0:T(8,128)(2,1)S(1)}, bf16[64,128]{1,0:T(8,128)(2,1)S(1)}, u32[]{:S(2)}, u32[]{:S(2)}) collective-permute-start(bf16[64,128]{1,0:T(8,128)(2,1)S(1)} %collective-permute-done.8), channel_id=1, source_target_pairs={{0,7},{1,0},{2,1},{3,2},{4,3},{5,4},{6,5},{7,6},{8,15},{9,8},{10,9... | collective-permute-start | bytes 49160 | tf_op jit(solution)/shard_map/ppermute | solution.py:61
  128.3 4.1 %collective-permute-start.11 = (bf16[64,128]{1,0:T(8,128)(2,1)S(1)}, bf16[64,128]{1,0:T(8,128)(2,1)S(1)}, u32[]{:S(2)}, u32[]{:S(2)}) collective-permute-start(bf16[64,128]{1,0:T(8,128)(2,1)S(1)} %collective-permute-done.9), channel_id=1, source_target_pairs={{0,1},{1,2},{2,3},{3,4},{4,5},{5,6},{6,7},{7,0},{8,9},{9,10},{10,1... | collective-permute-start | bytes 49160 | tf_op jit(solution)/shard_map/ppermute | solution.py:56
  128.4 4.1 %collective-permute-start.12 = (bf16[64,128]{1,0:T(8,128)(2,1)S(1)}, bf16[64,128]{1,0:T(8,128)(2,1)S(1)}, u32[]{:S(2)}, u32[]{:S(2)}) collective-permute-start(bf16[64,128]{1,0:T(8,128)(2,1)S(1)} %collective-permute-done.10), channel_id=1, source_target_pairs={{0,7},{1,0},{2,1},{3,2},{4,3},{5,4},{6,5},{7,6},{8,15},{9,8},{10,9... | collective-permute-start | bytes 49160 | tf_op jit(solution)/shard_map/ppermute | solution.py:61
  132.3 4.1 %collective-permute-start.13 = (bf16[64,128]{1,0:T(8,128)(2,1)S(1)}, bf16[64,128]{1,0:T(8,128)(2,1)S(1)}, u32[]{:S(2)}, u32[]{:S(2)}) collective-permute-start(bf16[64,128]{1,0:T(8,128)(2,1)S(1)} %collective-permute-done.11), channel_id=1, source_target_pairs={{0,1},{1,2},{2,3},{3,4},{4,5},{5,6},{6,7},{7,0},{8,9},{9,10},{10,1... | collective-permute-start | bytes 49160 | tf_op jit(solution)/shard_map/ppermute | solution.py:56
  136.4 0.9 copy-start.9
  141.2 62.1 %reduce-scatter.22.cloned.1.call-start = ((), (), s32[]{:S(2)}) async-start(), calls=%async_computation.8 | async-start | bytes 163840
  158.2 6.8 %copy-start.5 = (bf16[2,64,1536]{2,1,0:T(8,128)(2,1)S(1)}, bf16[2,64,1536]{2,1,0:T(8,128)(2,1)}, u32[]{:S(2)}) copy-start(bf16[2,64,1536]{2,1,0:T(8,128)(2,1)} %param.9) | copy-start | bytes 1179652
  158.2 24.5 %copy-start.7 = (pred[1024,512]{1,0:T(32,128)(4,1)S(1)}, pred[1024,512]{1,0:T(32,128)(4,1)}, u32[]{:S(2)}) copy-start(pred[1024,512]{1,0:T(32,128)(4,1)} %broadcast_in_dim.38) | copy-start | bytes 1572868
  166.3 4.1 %collective-permute-start.14 = (bf16[64,128]{1,0:T(8,128)(2,1)S(1)}, bf16[64,128]{1,0:T(8,128)(2,1)S(1)}, u32[]{:S(2)}, u32[]{:S(2)}) collective-permute-start(bf16[64,128]{1,0:T(8,128)(2,1)S(1)} %reshape.180), channel_id=1, source_target_pairs={{0,1},{1,2},{2,3},{3,4},{4,5},{5,6},{6,7},{7,0},{8,9},{9,10},{10,1... | collective-permute-start | bytes 49160 | tf_op jit(solution)/shard_map/ppermute | solution.py:56
  166.4 4.1 %collective-permute-start.15 = (bf16[64,128]{1,0:T(8,128)(2,1)S(1)}, bf16[64,128]{1,0:T(8,128)(2,1)S(1)}, u32[]{:S(2)}, u32[]{:S(2)}) collective-permute-start(bf16[64,128]{1,0:T(8,128)(2,1)S(1)} %reshape.180), channel_id=1, source_target_pairs={{0,7},{1,0},{2,1},{3,2},{4,3},{5,4},{6,5},{7,6},{8,15},{9,8},{10,9... | collective-permute-start | bytes 49160 | tf_op jit(solution)/shard_map/ppermute | solution.py:61
  170.4 4.1 %collective-permute-start.16 = (bf16[64,128]{1,0:T(8,128)(2,1)S(1)}, bf16[64,128]{1,0:T(8,128)(2,1)S(1)}, u32[]{:S(2)}, u32[]{:S(2)}) collective-permute-start(bf16[64,128]{1,0:T(8,128)(2,1)S(1)} %collective-permute-done.14), channel_id=1, source_target_pairs={{0,1},{1,2},{2,3},{3,4},{4,5},{5,6},{6,7},{7,0},{8,9},{9,10},{10,1... | collective-permute-start | bytes 49160 | tf_op jit(solution)/shard_map/ppermute | solution.py:56
  170.5 4.1 %collective-permute-start.17 = (bf16[64,128]{1,0:T(8,128)(2,1)S(1)}, bf16[64,128]{1,0:T(8,128)(2,1)S(1)}, u32[]{:S(2)}, u32[]{:S(2)}) collective-permute-start(bf16[64,128]{1,0:T(8,128)(2,1)S(1)} %collective-permute-done.15), channel_id=1, source_target_pairs={{0,7},{1,0},{2,1},{3,2},{4,3},{5,4},{6,5},{7,6},{8,15},{9,8},{10,9... | collective-permute-start | bytes 49160 | tf_op jit(solution)/shard_map/ppermute | solution.py:61
  174.5 4.1 %collective-permute-start.18 = (bf16[64,128]{1,0:T(8,128)(2,1)S(1)}, bf16[64,128]{1,0:T(8,128)(2,1)S(1)}, u32[]{:S(2)}, u32[]{:S(2)}) collective-permute-start(bf16[64,128]{1,0:T(8,128)(2,1)S(1)} %collective-permute-done.16), channel_id=1, source_target_pairs={{0,1},{1,2},{2,3},{3,4},{4,5},{5,6},{6,7},{7,0},{8,9},{9,10},{10,1... | collective-permute-start | bytes 49160 | tf_op jit(solution)/shard_map/ppermute | solution.py:56
  174.6 4.1 %collective-permute-start.19 = (bf16[64,128]{1,0:T(8,128)(2,1)S(1)}, bf16[64,128]{1,0:T(8,128)(2,1)S(1)}, u32[]{:S(2)}, u32[]{:S(2)}) collective-permute-start(bf16[64,128]{1,0:T(8,128)(2,1)S(1)} %collective-permute-done.17), channel_id=1, source_target_pairs={{0,7},{1,0},{2,1},{3,2},{4,3},{5,4},{6,5},{7,6},{8,15},{9,8},{10,9... | collective-permute-start | bytes 49160 | tf_op jit(solution)/shard_map/ppermute | solution.py:61
  178.6 4.1 %collective-permute-start.20 = (bf16[64,128]{1,0:T(8,128)(2,1)S(1)}, bf16[64,128]{1,0:T(8,128)(2,1)S(1)}, u32[]{:S(2)}, u32[]{:S(2)}) collective-permute-start(bf16[64,128]{1,0:T(8,128)(2,1)S(1)} %collective-permute-done.18), channel_id=1, source_target_pairs={{0,1},{1,2},{2,3},{3,4},{4,5},{5,6},{6,7},{7,0},{8,9},{9,10},{10,1... | collective-permute-start | bytes 49160 | tf_op jit(solution)/shard_map/ppermute | solution.py:56
  186.4 58.7 %reduce-scatter.24.cloned.1.call-start = ((), (), s32[]{:S(2)}) async-start(), calls=%async_computation.9 | async-start | bytes 163840
  203.4 23.3 %copy-start.10 = (f32[64,512]{1,0:T(8,128)S(1)}, f32[64,512]{1,0:T(8,128)}, u32[]{:S(2)}) copy-start(f32[64,512]{1,0:T(8,128)} %fusion.50) | copy-start | bytes 393220
  203.4 23.3 %copy-start.11 = (f32[64,512]{1,0:T(8,128)S(1)}, f32[64,512]{1,0:T(8,128)}, u32[]{:S(2)}) copy-start(f32[64,512]{1,0:T(8,128)} %fusion.49) | copy-start | bytes 393220
  210.3 4.1 %collective-permute-start.21 = (bf16[64,128]{1,0:T(8,128)(2,1)S(1)}, bf16[64,128]{1,0:T(8,128)(2,1)S(1)}, u32[]{:S(2)}, u32[]{:S(2)}) collective-permute-start(bf16[64,128]{1,0:T(8,128)(2,1)S(1)} %reshape.182), channel_id=1, source_target_pairs={{0,1},{1,2},{2,3},{3,4},{4,5},{5,6},{6,7},{7,0},{8,9},{9,10},{10,1... | collective-permute-start | bytes 49160 | tf_op jit(solution)/shard_map/ppermute | solution.py:56
  210.4 4.1 %collective-permute-start.22 = (bf16[64,128]{1,0:T(8,128)(2,1)S(1)}, bf16[64,128]{1,0:T(8,128)(2,1)S(1)}, u32[]{:S(2)}, u32[]{:S(2)}) collective-permute-start(bf16[64,128]{1,0:T(8,128)(2,1)S(1)} %reshape.182), channel_id=1, source_target_pairs={{0,7},{1,0},{2,1},{3,2},{4,3},{5,4},{6,5},{7,6},{8,15},{9,8},{10,9... | collective-permute-start | bytes 49160 | tf_op jit(solution)/shard_map/ppermute | solution.py:61
  214.5 4.1 %collective-permute-start.23 = (bf16[64,128]{1,0:T(8,128)(2,1)S(1)}, bf16[64,128]{1,0:T(8,128)(2,1)S(1)}, u32[]{:S(2)}, u32[]{:S(2)}) collective-permute-start(bf16[64,128]{1,0:T(8,128)(2,1)S(1)} %collective-permute-done.21), channel_id=1, source_target_pairs={{0,1},{1,2},{2,3},{3,4},{4,5},{5,6},{6,7},{7,0},{8,9},{9,10},{10,1... | collective-permute-start | bytes 49160 | tf_op jit(solution)/shard_map/ppermute | solution.py:56
  214.5 4.1 %collective-permute-start.24 = (bf16[64,128]{1,0:T(8,128)(2,1)S(1)}, bf16[64,128]{1,0:T(8,128)(2,1)S(1)}, u32[]{:S(2)}, u32[]{:S(2)}) collective-permute-start(bf16[64,128]{1,0:T(8,128)(2,1)S(1)} %collective-permute-done.22), channel_id=1, source_target_pairs={{0,7},{1,0},{2,1},{3,2},{4,3},{5,4},{6,5},{7,6},{8,15},{9,8},{10,9... | collective-permute-start | bytes 49160 | tf_op jit(solution)/shard_map/ppermute | solution.py:61
  218.5 4.1 %collective-permute-start.25 = (bf16[64,128]{1,0:T(8,128)(2,1)S(1)}, bf16[64,128]{1,0:T(8,128)(2,1)S(1)}, u32[]{:S(2)}, u32[]{:S(2)}) collective-permute-start(bf16[64,128]{1,0:T(8,128)(2,1)S(1)} %collective-permute-done.23), channel_id=1, source_target_pairs={{0,1},{1,2},{2,3},{3,4},{4,5},{5,6},{6,7},{7,0},{8,9},{9,10},{10,1... | collective-permute-start | bytes 49160 | tf_op jit(solution)/shard_map/ppermute | solution.py:56
  218.6 4.1 %collective-permute-start.26 = (bf16[64,128]{1,0:T(8,128)(2,1)S(1)}, bf16[64,128]{1,0:T(8,128)(2,1)S(1)}, u32[]{:S(2)}, u32[]{:S(2)}) collective-permute-start(bf16[64,128]{1,0:T(8,128)(2,1)S(1)} %collective-permute-done.24), channel_id=1, source_target_pairs={{0,7},{1,0},{2,1},{3,2},{4,3},{5,4},{6,5},{7,6},{8,15},{9,8},{10,9... | collective-permute-start | bytes 49160 | tf_op jit(solution)/shard_map/ppermute | solution.py:61
  222.6 4.1 %collective-permute-start.27 = (bf16[64,128]{1,0:T(8,128)(2,1)S(1)}, bf16[64,128]{1,0:T(8,128)(2,1)S(1)}, u32[]{:S(2)}, u32[]{:S(2)}) collective-permute-start(bf16[64,128]{1,0:T(8,128)(2,1)S(1)} %collective-permute-done.25), channel_id=1, source_target_pairs={{0,1},{1,2},{2,3},{3,4},{4,5},{5,6},{6,7},{7,0},{8,9},{9,10},{10,1... | collective-permute-start | bytes 49160 | tf_op jit(solution)/shard_map/ppermute | solution.py:56
Sparse Core Ops, SparseCore 0:
  43.3 19.7 reduce-scatter.15
  93.7 16.8 reduce-scatter.17
  141.4 16.7 reduce-scatter.19
  186.5 16.8 reduce-scatter.21
  228.1 16.9 reduce-scatter.23
